TPU v7x, 256 devices: a whole 4x4x8 slice. The times are simulated.
256 devices in a mesh: section: 2 (over core), grp: 4 (over x), dev: 32 (over y, z).
Axes of the slice: x: 4, y: 4, z: 8, core: 2. Of those that a mesh axis runs over, the one named last changes fastest.
Arguments:
- frames: bfloat16 [4, 512, 512, 256], P('grp', 'dev', 'section'), may hold values from -6 to 6
- templates: bfloat16 [8192, 256], P('dev'), may hold values from -0.375 to 0.375
- pair_block: int32 [2, 4, 256], P('section', 'grp', 'dev'), may hold values from 0 to 63
- pair_tile: int32 [2, 4, 256], P('section', 'grp', 'dev'), may hold values from 0 to 3
- pair_count: int32 [2, 4, 32], P('section', 'grp', 'dev'), may hold values from 1 to 8, 128 in all within a row
- owner_order: int32 [8192], replicated, may hold values from 0 to 8191, each once
Outputs:
- quantities: float32 [4, 8192], P('grp', 'dev')
Inputs may be any that keep to these rules, and one draw needn't show every extreme that they name: `pair_count`: each device's count of live slots; the counts of one section half and run sum to half of all slots there, and one of them is 8. `owner_order`: A permutation of the precursors.
All inputs are finite; a program needn't handle non-finite values.
Results may differ from a plain program's by a relative error of at most 0.00037.
Values may be sent and summed in bfloat16 or wider, within the bound.
A program may use at most 64 MiB of HBM per device.

v0:
```python
import math
import jax
import jax.numpy as jnp
from jax import lax
from jax.sharding import PartitionSpec as P

MOB = 512
SCALES = 6
RAD = 4
TM = 64
PB = 128
PREC = 8192
retention_spread = 2.0


def extended(cells, sides, width):
    for axis, dim in sides:
        count = lax.axis_size(axis)
        ends = count - 1
        head = lax.slice_in_dim(cells, 0, width, axis=dim)
        tail = lax.slice_in_dim(cells, cells.shape[dim] - width, cells.shape[dim], axis=dim)
        cells = jnp.concatenate(
            [
                lax.ppermute(tail, axis, [(i, (i + 1) % count) for i in range(ends)]),
                cells,
                lax.ppermute(head, axis, [((i + 1) % count, i) for i in range(ends)]),
            ],
            axis=dim,
        )
    return cells


def retention_weights():
    bell_values = [
        math.exp(-0.5 * (offset / retention_spread) ** 2) for offset in range(-RAD, RAD + 1)
    ]
    bell_total = sum(bell_values)
    return [weight_value / bell_total for weight_value in bell_values]


def mobility_kernels(row_start, row_count):
    row_place = (row_start + jnp.arange(row_count, dtype=jnp.int32)).astype(jnp.float32)
    col_place = jnp.arange(MOB, dtype=jnp.int32).astype(jnp.float32)
    distance = row_place[:, None] - col_place[None, :]
    tables = []
    for level in range(SCALES):
        spread_scans = 2.0**level
        scaled = distance / spread_scans
        tables.append(
            (1.0 - scaled * scaled)
            * jnp.exp(-0.5 * scaled * scaled)
            / math.sqrt(0.75 * math.sqrt(math.pi) * spread_scans)
        )
    return jnp.stack(tables).astype(jnp.bfloat16)


def on_device(frames, templates, pair_block, pair_tile, pair_count, owner_order):
    section_index = lax.axis_index("section")
    weights = retention_weights()
    count_frames = frames.shape[1]
    mob_local = frames.shape[2]
    channels = frames.shape[3]
    framed = extended(frames, (("dev", 1),), RAD)
    padded = framed.astype(jnp.float32)
    smoothed = weights[0] * padded[:, 0:count_frames]
    for offset in range(1, 2 * RAD + 1):
        smoothed = smoothed + weights[offset] * padded[:, offset : offset + count_frames]
    smoothed = smoothed.astype(jnp.bfloat16)
    gathered = lax.all_gather(smoothed, "section", axis=2, tiled=True)
    kernels = mobility_kernels(section_index * mob_local, mob_local)
    wavelet_stack = jnp.einsum(
        "smn,fnc->smfc", kernels, gathered[0], preferred_element_type=jnp.float32
    ).astype(jnp.bfloat16)
    template_panel = lax.all_gather(templates, "dev", axis=0, tiled=True)
    blocks = template_panel.shape[0] // PB
    live_pairs = pair_count[0, 0, 0]
    block_ids = pair_block[0, 0]
    tile_ids = pair_tile[0, 0]

    def visit_pair(slot_index, totals):
        block_id = block_ids[slot_index]
        tile_id = tile_ids[slot_index]
        tile_cells = lax.dynamic_slice_in_dim(wavelet_stack, tile_id * TM, TM, 1).reshape(
            -1, channels
        )
        block_rows = lax.dynamic_slice_in_dim(template_panel, block_id * PB, PB, 0)
        scores = jnp.dot(tile_cells, block_rows.T, preferred_element_type=jnp.float32)
        response = jnp.mean(jnp.maximum(scores, 0.0), axis=0)
        block_hit = (jnp.arange(blocks, dtype=jnp.int32) == block_id).astype(jnp.float32)
        return totals + block_hit[:, None] * response[None, :]

    totals = lax.fori_loop(0, live_pairs, visit_pair, jnp.zeros((blocks, PB), jnp.float32))
    placed = jnp.zeros((PREC,), jnp.float32).at[owner_order].set(totals.reshape(-1))[None]
    summed = lax.psum(placed, "section")
    owned = lax.psum_scatter(summed, "dev", scatter_dimension=1, tiled=True)
    run_count = lax.axis_size("grp")
    run_mask = (jnp.arange(run_count, dtype=jnp.int32) == lax.axis_index("grp")).astype(jnp.float32)
    run_totals = lax.psum(run_mask * jnp.sum(owned), ("grp", "dev"))
    own_total = jnp.sum(run_totals * run_mask)
    factor = jnp.mean(run_totals) / own_total
    return owned * factor


def solution(mesh):
    placed = (
        P("grp", "dev", "section", None),
        P("dev", None),
        P("section", "grp", "dev"),
        P("section", "grp", "dev"),
        P("section", "grp", "dev"),
        P(),
    )
    return jax.shard_map(
        on_device, mesh=mesh, in_specs=placed, out_specs=P("grp", "dev"), check_vma=False
    )
```

profile of v0, /device:TPU:0, one launch (start us, length us, event | category | flops | bytes accessed | tf_op | source)
XLA Modules:
  0.0 833.9 jit_solution(16655650894832102042)
XLA Ops:
  6.5 0.0 all-gather.3.cloned.1.call-start
  6.5 1.3 fusion.63
  7.8 2.1 collective-permute-start
  9.9 1.3 collective-permute-start.1
  11.2 9.8 %collective-permute-done = bf16[1,4,256,256]{3,2,1,0:T(8,128)(2,1)S(1)} collective-permute-done((bf16[1,4,256,256]{3,2,1,0:T(8,128)(2,1)S(1)}, bf16[1,4,256,256]{3,2,1,0:T(8,128)(2,1)S(1)}, u32[]{:S(2)}, u32[]{:S(2)}) %collective-permute-start) | collective-permute-done | bytes 524320 | tf_op jit(solution)/shard_map/ppermute | solution.py:24
  21.1 4.3 collective-permute-done.1
  25.4 2.1 maximum_convert_fusion
  27.4 0.0 copy-start
  27.4 5.7 fusion.4
  33.1 0.0 all-gather.3.cloned.1.call-update
  33.2 0.0 all-gather.5.cloned.1.call-start
  33.2 0.7 all-gather.5.cloned.1.call-update
  33.9 0.0 reduce-scatter.4.cloned.1.call-start
  34.0 0.0 copy-done
  34.0 0.2 fusion.59
  34.3 0.3 fusion.54
  34.5 0.3 fusion.55
  34.8 0.3 fusion.56
  35.0 0.3 fusion.57
  35.3 0.3 fusion.58
  35.5 0.0 copy-start.1
  35.6 0.0 copy-start.2
  35.6 19.7 %all-gather.3.cloned.1.call-done = bf16[1,16,512,256]{3,2,1,0:T(8,128)(2,1)} async-done(((bf16[1,16,256,256]{3,2,1,0:T(8,128)(2,1)}), bf16[1,16,512,256]{3,2,1,0:T(8,128)(2,1)}) %all-gather.3.cloned.1.call-update) | async-done | bytes 4194320 | tf_op jit(solution)/shard_map/all_gather | solution.py:69
  55.2 11.7 %convolution_convert_fusion = bf16[6,256,16,256]{3,1,2,0:T(8,128)(2,1)} fusion(bf16[1,16,512,256]{3,2,1,0:T(8,128)(2,1)} %all-gather.3.cloned.1.call-done, bf16[6,256,512]{2,1,0:T(8,128)(2,1)S(1)} %fusion.58), kind=kOutput, calls=%fused_computation.9 | convolution fusion | flops 6448742400 | bytes 18350080 | tf_op jit(solution)/shard_map/smn,fnc->smfc/dot_general | solution.py:71
  66.9 73.7 %all-gather.5.cloned.1.call-done = bf16[8192,256]{1,0:T(8,128)(2,1)} async-done(((bf16[256,256]{1,0:T(8,128)(2,1)}), bf16[8192,256]{1,0:T(8,128)(2,1)}) %all-gather.5.cloned.1.call-update) | async-done | bytes 4194320 | tf_op jit(solution)/shard_map/all_gather | solution.py:74
  140.7 0.0 copy-done.1
  140.7 0.0 copy-done.2
  140.7 10.7 %while.10 = (s32[]{:T(128)}, f32[64,128]{1,0:T(8,128)S(1)}, s32[]{:T(128)}, s32[8]{0:T(128)S(1)}, s32[8]{0:T(128)S(1)}, /*index=5*/bf16[6,256,16,256]{3,1,2,0:T(...) while((s32[]{:T(128)}, f32[64,128]{1,0:T(8,128)S(1)}, ...), condition=%wide.region_2.0_spmd, body=%wide.region_0.0_spmd.sunk | while | flops 404242560 | bytes 15862567 | solution.py:92
  141.4 0.6 dynamic_slice.21
  142.5 2.3 constant_dynamic-slice_fusion.2
  144.8 1.9 copy.14
  146.7 0.6 dynamic_slice.22
  147.9 2.2 fusion.70
  150.1 0.6 compare_convert_fusion.2
  150.7 0.1 multiply_add_fusion.2
  151.4 30.5 %scatter_custom_fusion = f32[8192]{0:T(1024)S(1)} fusion(s32[8192]{0:T(1024)S(1)} %compare_select_fusion, f32[8192]{0:T(1024)S(1)} %bitcast.30, f32[]{:T(128)} %constant.32.clone.1), kind=kCustom, calls=%fused_computation.91 | custom fusion | bytes 32772 | tf_op jit(solution)/shard_map/scatter | solution.py:93
  181.9 2.6 copy.10
  184.5 0.0 reduce-scatter.4.cloned.1.call-update
  184.6 288.7 %reduce-scatter.4.cloned.1.call-done = f32[256,1]{1,0:T(8,128)} async-done(((f32[8192,1]{1,0:T(8,128)}), f32[256,1]{1,0:T(8,128)}) %reduce-scatter.4.cloned.1.call-update) | async-done | bytes 1040
  473.2 1.0 copy.11
  474.2 2.5 psum.16
  476.7 0.6 reduce_sum.36
  477.3 0.6 compare_select_fusion.2
  477.9 346.8 %psum.15 = f32[4]{0:T(128)S(1)} all-reduce(f32[4]{0:T(128)S(1)} %compare_select_fusion.2), channel_id=1, replica_groups=mesh['section'=2,'grp'=4,'dev'=32] {'grp','dev'}, use_global_device_ids=true, to_apply=%region_7.0 | all-reduce | flops 4 | bytes 32 | tf_op jit(solution)/shard_map/psum | solution.py:98
  824.8 0.7 fusion.62
  826.8 0.6 broadcast_multiply_fusion.1
  (5 shorter events, 0.0 us)
Async XLA Ops:
  6.5 48.7 %all-gather.3.cloned.1.call-start = ((), (), s32[]{:S(2)}) async-start(), calls=%async_computation.1 | async-start | bytes 6291456 | tf_op jit(solution)/shard_map/all_gather | solution.py:69
  7.8 13.3 %collective-permute-start = (bf16[1,4,256,256]{3,2,1,0:T(8,128)(2,1)S(1)}, bf16[1,4,256,256]{3,2,1,0:T(8,128)(2,1)S(1)}, u32[]{:S(2)}, u32[]{:S(2)}) collective-permute-start(bf16[1,4,256,256]{3,2,1,0:T(8,128)(2,1)S(1)} %get-tuple-element.74), channel_id=1, source_target_pairs={{0,1},{1,2},{2,3},{3,4},{4,5},{5,6},{6,7},{7,8},{8,9},{9,10},{10,1... | collective-permute-start | bytes 1572872 | tf_op jit(solution)/shard_map/ppermute | solution.py:24
  9.9 15.4 %collective-permute-start.1 = (bf16[1,4,256,256]{3,2,1,0:T(8,128)(2,1)S(1)}, bf16[1,4,256,256]{3,2,1,0:T(8,128)(2,1)S(1)}, u32[]{:S(2)}, u32[]{:S(2)}) collective-permute-start(bf16[1,4,256,256]{3,2,1,0:T(8,128)(2,1)S(1)} %get-tuple-element.75), channel_id=1, source_target_pairs={{1,0},{2,1},{3,2},{4,3},{5,4},{6,5},{7,6},{8,7},{9,8},{10,9},{11,1... | collective-permute-start | bytes 1572872 | tf_op jit(solution)/shard_map/ppermute | solution.py:26
  27.4 6.6 copy-start
  33.2 107.5 %all-gather.5.cloned.1.call-start = ((), (), s32[]{:S(2)}) async-start(), calls=%async_computation.2 | async-start | bytes 4325376 | tf_op jit(solution)/shard_map/all_gather | solution.py:74
  33.9 439.3 %reduce-scatter.4.cloned.1.call-start = ((), (), s32[]{:S(2)}) async-start(), calls=%async_computation.3 | async-start | bytes 4325376
  35.5 105.1 %copy-start.1 = (s32[1,1,8]{2,1,0:T(1,128)S(1)}, s32[1,1,8]{2,1,0:T(1,128)}, u32[]{:S(2)}) copy-start(s32[1,1,8]{2,1,0:T(1,128)} %param.10) | copy-start | bytes 100
  35.6 105.1 %copy-start.2 = (s32[1,1,8]{2,1,0:T(1,128)S(1)}, s32[1,1,8]{2,1,0:T(1,128)}, u32[]{:S(2)}) copy-start(s32[1,1,8]{2,1,0:T(1,128)} %param.11) | copy-start | bytes 100
Sparse Core Ops, SparseCore 0:
  33.3 21.9 all-gather.2
  57.8 82.8 all-gather.4
  184.7 288.5 reduce-scatter.3
where the time goes:
time: 835 us; the launch traced here: 834 us
  waiting for transfers between devices  397 us (48%)
  blocking collectives  349 us (42%)
  local copies, waits for them, and re-layouts  40.7 us (5%)
  between operations  14.6 us (2%)
  matrix products  13.9 us (2%)
  other arithmetic  12.4 us (1%)
    psum x1, blocking collectives, on_device(): run_totals = lax.psum(run_mask * jnp.sum(owned), ('grp', 'dev'))  347 us
    unnamed x4, waiting for transfers between devices  289 us
    all_gather x1, waiting for transfers between devices, on_device(): template_panel = lax.all_gather(templates, 'dev', axis=0, tiled=True)  73.7 us
    scatter x1, local copies, waits for them, and re-layouts, on_device(): jnp.zeros((PREC,), jnp.float32).at[owner_order].set(totals.reshape(-1))  30.5 us
    all_gather x1, waiting for transfers between devices, on_device(): gathered = lax.all_gather(smoothed, 'section', axis=2, tiled=True)  19.7 us
  transfers between devices with their start and end apart: 5, of which 5 were waited for; matrix products, arithmetic and copies ran while one was open for 2% of the time, Pallas kernels for 0%

commit v1 on v0

--- a/solution.py
+++ b/solution.py
@@ -3,6 +3,7 @@
 import jax.numpy as jnp
 from jax import lax
 from jax.sharding import PartitionSpec as P
+from jax.lax import psum
 
 MOB = 512
 SCALES = 6
@@ -11,6 +12,12 @@
 PB = 128
 PREC = 8192
 retention_spread = 2.0
+
+
+def point_the_shapes(original, mesh_dim, lane_axis):
+    for idx in (mesh_dim, lane_axis):
+        original = psum(original, idx)
+    return original
 
 
 def extended(cells, sides, width):
@@ -95,7 +102,7 @@
     owned = lax.psum_scatter(summed, "dev", scatter_dimension=1, tiled=True)
     run_count = lax.axis_size("grp")
     run_mask = (jnp.arange(run_count, dtype=jnp.int32) == lax.axis_index("grp")).astype(jnp.float32)
-    run_totals = lax.psum(run_mask * jnp.sum(owned), ("grp", "dev"))
+    run_totals = point_the_shapes(run_mask * jnp.sum(owned), "grp", "dev")
     own_total = jnp.sum(run_totals * run_mask)
     factor = jnp.mean(run_totals) / own_total
     return owned * factor

time: 835 us -> 571 us (0.68)
  blocking collectives: 349 us -> 85.1 us
    psum x1 -> x2, blocking collectives: 347 us -> 82.6 us  [point_the_shapes(): original = psum(original, idx)]
where the time goes in v1:
time: 571 us; the launch traced here: 570 us
  waiting for transfers between devices  397 us (70%)
  blocking collectives  85.1 us (15%)
  local copies, waits for them, and re-layouts  40.7 us (7%)
  between operations  14.6 us (3%)
  matrix products  13.9 us (2%)
  other arithmetic  12.4 us (2%)
    unnamed x4, waiting for transfers between devices  289 us
    psum x2, blocking collectives, point_the_shapes(): original = psum(original, idx)  82.6 us
    all_gather x1, waiting for transfers between devices, on_device(): template_panel = lax.all_gather(templates, 'dev', axis=0, tiled=True)  73.7 us
    scatter x1, local copies, waits for them, and re-layouts, on_device(): jnp.zeros((PREC,), jnp.float32).at[owner_order].set(totals.reshape(-1))  30.5 us
    all_gather x1, waiting for transfers between devices, on_device(): gathered = lax.all_gather(smoothed, 'section', axis=2, tiled=True)  19.7 us
    dot_general x1, matrix products, on_device(): jnp.einsum('smn,fnc->smfc', kernels, gathered[0], preferred_element_type=...  11.7 us
  transfers between devices with their start and end apart: 5, of which 5 were waited for; matrix products, arithmetic and copies ran while one was open for 2% of the time, Pallas kernels for 0%

profile of v1, /device:TPU:0, one launch (start us, length us, event | category | flops | bytes accessed | tf_op | source)
XLA Modules:
  0.0 569.7 jit_solution(2481325818425955099)
XLA Ops:
  6.5 0.0 all-gather.3.cloned.1.call-start
  6.5 1.3 fusion.63
  7.8 2.1 collective-permute-start
  9.9 1.3 collective-permute-start.1
  11.2 9.8 %collective-permute-done = bf16[1,4,256,256]{3,2,1,0:T(8,128)(2,1)S(1)} collective-permute-done((bf16[1,4,256,256]{3,2,1,0:T(8,128)(2,1)S(1)}, bf16[1,4,256,256]{3,2,1,0:T(8,128)(2,1)S(1)}, u32[]{:S(2)}, u32[]{:S(2)}) %collective-permute-start) | collective-permute-done | bytes 524320 | tf_op jit(solution)/shard_map/ppermute | solution.py:31
  21.1 4.3 collective-permute-done.1
  25.4 2.1 maximum_convert_fusion
  27.4 0.0 copy-start
  27.4 5.7 %fusion.4 = bf16[1,16,256,256]{3,2,1,0:T(8,128)(2,1)} fusion(f32[1,24,256,256]{3,2,1,0:T(8,128)S(1)} %maximum_convert_fusion), kind=kLoop, calls=%fused_computation.12 | loop fusion | flops 18874368 | bytes 39845888 | tf_op jit(solution)/shard_map/convert_element_type | solution.py:75
  33.1 0.0 all-gather.3.cloned.1.call-update
  33.2 0.0 all-gather.5.cloned.1.call-start
  33.2 0.7 all-gather.5.cloned.1.call-update
  33.9 0.0 reduce-scatter.4.cloned.1.call-start
  34.0 0.0 copy-done
  34.0 0.2 fusion.59
  34.3 0.3 fusion.54
  34.5 0.3 fusion.55
  34.8 0.3 fusion.56
  35.0 0.3 fusion.57
  35.3 0.3 fusion.58
  35.5 0.0 copy-start.1
  35.6 0.0 copy-start.2
  35.6 19.7 %all-gather.3.cloned.1.call-done = bf16[1,16,512,256]{3,2,1,0:T(8,128)(2,1)} async-done(((bf16[1,16,256,256]{3,2,1,0:T(8,128)(2,1)}), bf16[1,16,512,256]{3,2,1,0:T(8,128)(2,1)}) %all-gather.3.cloned.1.call-update) | async-done | bytes 4194320 | tf_op jit(solution)/shard_map/all_gather | solution.py:76
  55.2 11.7 %convolution_convert_fusion = bf16[6,256,16,256]{3,1,2,0:T(8,128)(2,1)} fusion(bf16[1,16,512,256]{3,2,1,0:T(8,128)(2,1)} %all-gather.3.cloned.1.call-done, bf16[6,256,512]{2,1,0:T(8,128)(2,1)S(1)} %fusion.58), kind=kOutput, calls=%fused_computation.9 | convolution fusion | flops 6448742400 | bytes 18350080 | tf_op jit(solution)/shard_map/smn,fnc->smfc/dot_general | solution.py:78
  66.9 73.7 %all-gather.5.cloned.1.call-done = bf16[8192,256]{1,0:T(8,128)(2,1)} async-done(((bf16[256,256]{1,0:T(8,128)(2,1)}), bf16[8192,256]{1,0:T(8,128)(2,1)}) %all-gather.5.cloned.1.call-update) | async-done | bytes 4194320 | tf_op jit(solution)/shard_map/all_gather | solution.py:81
  140.7 0.0 copy-done.1
  140.7 0.0 copy-done.2
  140.7 10.7 %while.10 = (s32[]{:T(128)}, f32[64,128]{1,0:T(8,128)S(1)}, s32[]{:T(128)}, s32[8]{0:T(128)S(1)}, s32[8]{0:T(128)S(1)}, /*index=5*/bf16[6,256,16,256]{3,1,2,0:T(...) while((s32[]{:T(128)}, f32[64,128]{1,0:T(8,128)S(1)}, ...), condition=%wide.region_2.0_spmd, body=%wide.region_0.0_spmd.sunk | while | flops 404242560 | bytes 15862567 | solution.py:99
  141.4 0.6 dynamic_slice.21
  142.5 2.3 constant_dynamic-slice_fusion.2
  144.8 1.9 copy.14
  146.7 0.6 dynamic_slice.22
  147.9 2.2 fusion.70
  150.1 0.6 compare_convert_fusion.2
  150.7 0.1 multiply_add_fusion.2
  151.4 30.5 %scatter_custom_fusion = f32[8192]{0:T(1024)S(1)} fusion(s32[8192]{0:T(1024)S(1)} %compare_select_fusion, f32[8192]{0:T(1024)S(1)} %bitcast.30, f32[]{:T(128)} %constant.32.clone.1), kind=kCustom, calls=%fused_computation.91 | custom fusion | bytes 32772 | tf_op jit(solution)/shard_map/scatter | solution.py:100
  181.9 2.6 copy.10
  184.5 0.0 reduce-scatter.4.cloned.1.call-update
  184.6 288.7 %reduce-scatter.4.cloned.1.call-done = f32[256,1]{1,0:T(8,128)} async-done(((f32[8192,1]{1,0:T(8,128)}), f32[256,1]{1,0:T(8,128)}) %reduce-scatter.4.cloned.1.call-update) | async-done | bytes 1040
  473.2 1.0 copy.11
  474.2 2.5 psum.24
  476.7 0.6 reduce_sum.36
  477.3 0.6 compare_select_fusion.2
  477.9 10.4 %psum.22 = f32[4]{0:T(128)S(1)} all-reduce(f32[4]{0:T(128)S(1)} %compare_select_fusion.2), channel_id=1, replica_groups=mesh['section'=2,'grp'=4,'dev'=32] {'grp'}, use_global_device_ids=true, to_apply=%region_7.0 | all-reduce | flops 4 | bytes 32 | tf_op jit(solution)/shard_map/psum | solution.py:19
  488.4 72.2 %psum.23 = f32[4]{0:T(128)S(1)} all-reduce(f32[4]{0:T(128)S(1)} %psum.22), channel_id=1, replica_groups=mesh['section'=2,'grp'=4,'dev'=32] {'dev'}, use_global_device_ids=true, to_apply=%region_8.0 | all-reduce | flops 4 | bytes 32 | tf_op jit(solution)/shard_map/psum | solution.py:19
  560.5 0.7 fusion.62
  562.6 0.6 broadcast_multiply_fusion.1
  (5 shorter events, 0.0 us)
Async XLA Ops:
  6.5 48.7 %all-gather.3.cloned.1.call-start = ((), (), s32[]{:S(2)}) async-start(), calls=%async_computation.1 | async-start | bytes 6291456 | tf_op jit(solution)/shard_map/all_gather | solution.py:76
  7.8 13.3 %collective-permute-start = (bf16[1,4,256,256]{3,2,1,0:T(8,128)(2,1)S(1)}, bf16[1,4,256,256]{3,2,1,0:T(8,128)(2,1)S(1)}, u32[]{:S(2)}, u32[]{:S(2)}) collective-permute-start(bf16[1,4,256,256]{3,2,1,0:T(8,128)(2,1)S(1)} %get-tuple-element.74), channel_id=1, source_target_pairs={{0,1},{1,2},{2,3},{3,4},{4,5},{5,6},{6,7},{7,8},{8,9},{9,10},{10,1... | collective-permute-start | bytes 1572872 | tf_op jit(solution)/shard_map/ppermute | solution.py:31
  9.9 15.4 %collective-permute-start.1 = (bf16[1,4,256,256]{3,2,1,0:T(8,128)(2,1)S(1)}, bf16[1,4,256,256]{3,2,1,0:T(8,128)(2,1)S(1)}, u32[]{:S(2)}, u32[]{:S(2)}) collective-permute-start(bf16[1,4,256,256]{3,2,1,0:T(8,128)(2,1)S(1)} %get-tuple-element.75), channel_id=1, source_target_pairs={{1,0},{2,1},{3,2},{4,3},{5,4},{6,5},{7,6},{8,7},{9,8},{10,9},{11,1... | collective-permute-start | bytes 1572872 | tf_op jit(solution)/shard_map/ppermute | solution.py:33
  27.4 6.6 %copy-start = (s32[8192]{0:T(1024)S(1)}, s32[8192]{0:T(1024)}, u32[]{:S(2)}) copy-start(s32[8192]{0:T(1024)} %param.13) | copy-start | bytes 98308
  33.2 107.5 %all-gather.5.cloned.1.call-start = ((), (), s32[]{:S(2)}) async-start(), calls=%async_computation.2 | async-start | bytes 4325376 | tf_op jit(solution)/shard_map/all_gather | solution.py:81
  33.9 439.3 %reduce-scatter.4.cloned.1.call-start = ((), (), s32[]{:S(2)}) async-start(), calls=%async_computation.3 | async-start | bytes 4325376
  35.5 105.1 %copy-start.1 = (s32[1,1,8]{2,1,0:T(1,128)S(1)}, s32[1,1,8]{2,1,0:T(1,128)}, u32[]{:S(2)}) copy-start(s32[1,1,8]{2,1,0:T(1,128)} %param.10) | copy-start | bytes 100
  35.6 105.1 %copy-start.2 = (s32[1,1,8]{2,1,0:T(1,128)S(1)}, s32[1,1,8]{2,1,0:T(1,128)}, u32[]{:S(2)}) copy-start(s32[1,1,8]{2,1,0:T(1,128)} %param.11) | copy-start | bytes 100
Sparse Core Ops, SparseCore 0:
  33.3 21.9 all-gather.2
  57.8 82.8 all-gather.4
  184.7 288.5 reduce-scatter.3
